TPU v7x, 128 devices: a whole 4x4x4 slice. The times are simulated.
128 devices in a mesh: group: 4 (over z_lo, core), dp: 2 (over z_hi), tensor: 16 (over x, y).
Axes of the slice: x: 4, y: 4, z: 4 (z_hi: 2, z_lo: 2; z = z_hi * 2 + z_lo), core: 2. Of those that a mesh axis runs over, the one named last changes fastest.
Arguments:
- tokens: bfloat16 [2048, 8, 2048], P('tensor', ('group', 'dp')), may hold values from -6 to 6
- cotangent: bfloat16 [2048, 8, 2048], P('tensor', ('group', 'dp')), may hold values from -6 to 6
- lengths: int32 [8], replicated, may hold values from 1 to 2048, 9830 in all
- ln1_gain: float32 [2048], replicated, may hold values from 0.25 to 1.75
- ln1_bias: float32 [2048], replicated, may hold values from -1.75 to 1.75
- w_qkv: bfloat16 [2048, 3, 16, 128], P(None, None, 'tensor'), may hold values from -0.125 to 0.125
- b_qv: float32 [2, 2048], P(None, 'tensor'), may hold values from -1.75 to 1.75
- w_o: bfloat16 [16, 128, 2048], P('tensor'), may hold values from -0.75 to 0.75
- b_o: float32 [2048], replicated, may hold values from -1.75 to 1.75
- ln2_gain: float32 [2048], replicated, may hold values from 0.25 to 1.75
- ln2_bias: float32 [2048], replicated, may hold values from -1.75 to 1.75
- w_in: bfloat16 [2048, 8192], P(None, 'tensor'), may hold values from -0.125 to 0.125
- b_in: float32 [8192], P('tensor'), may hold values from -1.75 to 1.75
- w_out: bfloat16 [8192, 2048], P('tensor'), may hold values from -0.0625 to 0.0625
- b_out: float32 [2048], replicated, may hold values from -1.75 to 1.75
Outputs:
- output: bfloat16 [2048, 8, 2048], P('tensor', ('group', 'dp'))
- input_grad: bfloat16 [2048, 8, 2048], P('tensor', ('group', 'dp'))
- d_ln1_gain: float32 [2048], P(('group', 'dp', 'tensor'))
- d_ln1_bias: float32 [2048], P(('group', 'dp', 'tensor'))
- d_w_qkv: float32 [2048, 3, 16, 128], P(('group', 'dp'), None, 'tensor')
- d_b_qv: float32 [2, 2048], P(None, ('group', 'dp', 'tensor'))
- d_w_o: float32 [16, 128, 2048], P('tensor', None, ('group', 'dp'))
- d_b_o: float32 [2048], P(('group', 'dp', 'tensor'))
- d_ln2_gain: float32 [2048], P(('group', 'dp', 'tensor'))
- d_ln2_bias: float32 [2048], P(('group', 'dp', 'tensor'))
- d_w_in: float32 [2048, 8192], P(('group', 'dp'), 'tensor')
- d_b_in: float32 [8192], P(('group', 'dp', 'tensor'))
- d_w_out: float32 [8192, 2048], P('tensor', ('group', 'dp'))
- d_b_out: float32 [2048], P(('group', 'dp', 'tensor'))
Inputs may be any that keep to these rules, and one draw needn't show every extreme that they name: The true lengths of the 8 sequences sum to 9830.
All inputs are finite; a program needn't handle non-finite values.
Results may differ from a plain program's by a relative error of at most 0.02.
Values may be sent and summed in bfloat16 or wider, within the bound.
No kernel may reach another device: no remote copies, remote signals or barrier semaphores. Data moves between devices by JAX's collectives and lax.ppermute only.
A program may use at most 192 MiB of HBM per device.

v0:
```python
from functools import partial
import math
import jax
import jax.numpy as jnp
from jax import lax
from jax.sharding import PartitionSpec as P

EPS = 1e-05
NEGATIVE = -1e30


def layer_norm(value, gain, shift):
    mean = jnp.mean(value, axis=-1, keepdims=True)
    centred = value - mean
    spread = jnp.mean(centred * centred, axis=-1, keepdims=True)
    return centred * lax.rsqrt(spread + EPS) * gain + shift


def gelu_tanh(value):
    return jax.nn.gelu(value, approximate=True)


def block_scores(rows_query, key_rows, first, length, score_scale):
    count = rows_query.shape[0]
    key_pos = jnp.arange(key_rows.shape[0], dtype=jnp.int32)
    query_pos = first + jnp.arange(count, dtype=jnp.int32)
    valid = (key_pos[None, :] <= query_pos[:, None]) & (key_pos[None, :] < length)
    scores = (
        lax.dot_general(
            rows_query, key_rows, (((1,), (1,)), ((), ())), preferred_element_type=jnp.float32
        )
        * score_scale
    )
    return (jnp.where(valid, scores, NEGATIVE), valid)


def attend_forward(item, block_rows, score_scale):
    query, key_rows, value_rows, length = item
    outputs = []
    log_parts = []
    for first in range(0, query.shape[0], block_rows):
        rows_query = query[first : first + block_rows]
        scores, valid = block_scores(rows_query, key_rows, first, length, score_scale)
        peak = jnp.max(scores, axis=-1, keepdims=True)
        expo = jnp.exp(scores - peak)
        weight_sum = jnp.sum(expo, axis=-1, keepdims=True)
        probs = (expo / weight_sum).astype(jnp.bfloat16)
        outputs.append(
            jnp.dot(probs, value_rows, preferred_element_type=jnp.float32).astype(jnp.bfloat16)
        )
        log_parts.append((peak + jnp.log(weight_sum))[:, 0])
    return (jnp.concatenate(outputs, 0), jnp.concatenate(log_parts, 0))


def attend_backward(item, block_rows, score_scale):
    query, key_rows, value_rows, length, grad_out, log_sums = item
    key_grad = jnp.zeros(key_rows.shape, jnp.float32)
    value_grad = jnp.zeros(value_rows.shape, jnp.float32)
    query_parts = []
    for first in range(0, query.shape[0], block_rows):
        rows_query = query[first : first + block_rows]
        scores, valid = block_scores(rows_query, key_rows, first, length, score_scale)
        probs = jnp.where(valid, jnp.exp(scores - log_sums[first : first + block_rows, None]), 0.0)
        grad_rows = grad_out[first : first + block_rows]
        probs_grad = lax.dot_general(
            grad_rows, value_rows, (((1,), (1,)), ((), ())), preferred_element_type=jnp.float32
        )
        inner = jnp.sum(probs * probs_grad, axis=-1, keepdims=True)
        score_grad = (probs * (probs_grad - inner)).astype(jnp.bfloat16)
        query_parts.append(
            jnp.dot(score_grad, key_rows, preferred_element_type=jnp.float32) * score_scale
        )
        key_grad = (
            key_grad
            + lax.dot_general(
                score_grad, rows_query, (((0,), (0,)), ((), ())), preferred_element_type=jnp.float32
            )
            * score_scale
        )
        value_grad = value_grad + lax.dot_general(
            probs.astype(jnp.bfloat16),
            grad_rows,
            (((0,), (0,)), ((), ())),
            preferred_element_type=jnp.float32,
        )
    return (
        jnp.concatenate(query_parts, 0).astype(jnp.bfloat16),
        key_grad.astype(jnp.bfloat16),
        value_grad.astype(jnp.bfloat16),
    )


def shards(
    tokens,
    cotangent,
    lengths,
    ln1_gain,
    ln1_bias,
    w_qkv,
    b_qv,
    w_o,
    b_o,
    ln2_gain,
    ln2_bias,
    w_in,
    b_in,
    w_out,
    b_out,
):
    row_count, seq_count, model_width = tokens.shape
    tensor_count = lax.axis_size("tensor")
    tensor_rank = lax.axis_index("tensor")
    seq_total = row_count * tensor_count
    local_heads = w_qkv.shape[2]
    head_size = w_qkv.shape[3]
    local_width = local_heads * head_size
    hidden = w_in.shape[1]
    block_rows = min(512, seq_total)
    score_scale = 1.0 / math.sqrt(head_size)
    group_count = lax.axis_size("group")
    group_rank = lax.axis_index("group")
    member = group_rank * lax.axis_size("dp") + lax.axis_index("dp")
    seq_lengths = lax.dynamic_slice_in_dim(lengths, member * seq_count, seq_count, 0)
    group_totals = jnp.sum(lengths.reshape(group_count, -1), axis=1).astype(jnp.float32)
    factor = (
        group_count
        * lax.dynamic_index_in_dim(group_totals, group_rank, 0, keepdims=False)
        / jnp.sum(group_totals)
    )
    inputs = tokens.astype(jnp.float32)
    normed_low = layer_norm(inputs, ln1_gain, ln1_bias).astype(jnp.bfloat16)
    normed_full = lax.all_gather(normed_low, "tensor", axis=0, tiled=True)
    joint_weight = w_qkv.reshape(model_width, 3 * local_width)
    projected = jnp.dot(
        normed_full.reshape(seq_total * seq_count, model_width),
        joint_weight,
        preferred_element_type=jnp.float32,
    )
    projected = projected.reshape(seq_total, seq_count, 3, local_width)
    query = (projected[:, :, 0] + b_qv[0]).astype(jnp.bfloat16)
    keys = projected[:, :, 1].astype(jnp.bfloat16)
    values = (projected[:, :, 2] + b_qv[1]).astype(jnp.bfloat16)

    def per_item(array):
        shaped = array.reshape(seq_total, seq_count, local_heads, head_size)
        return jnp.transpose(shaped, (1, 2, 0, 3)).reshape(
            seq_count * local_heads, seq_total, head_size
        )

    def per_row(array):
        shaped = array.reshape(seq_count, local_heads, seq_total, head_size)
        return jnp.transpose(shaped, (2, 0, 1, 3)).reshape(seq_total, seq_count, local_width)

    query_items = per_item(query)
    key_items = per_item(keys)
    value_items = per_item(values)
    item_lengths = jnp.repeat(seq_lengths, local_heads)
    heads_out, log_sums = lax.map(
        partial(attend_forward, block_rows=block_rows, score_scale=score_scale),
        (query_items, key_items, value_items, item_lengths),
    )
    attended = per_row(heads_out)
    out_weight = w_o.reshape(local_width, model_width)
    piece = attended
    attention = (
        lax.psum_scatter(
            jnp.einsum("rse,ed->rsd", piece, out_weight, preferred_element_type=jnp.float32),
            "tensor",
            scatter_dimension=0,
            tiled=True,
        )
        + b_o
    )
    middle = inputs + attention
    second_low = layer_norm(middle, ln2_gain, ln2_bias).astype(jnp.bfloat16)
    second_full = lax.all_gather(second_low, "tensor", axis=0, tiled=True)
    pre_act = (
        jnp.dot(
            second_full.reshape(seq_total * seq_count, model_width),
            w_in,
            preferred_element_type=jnp.float32,
        )
        + b_in
    )
    activated = gelu_tanh(pre_act).astype(jnp.bfloat16).reshape(seq_total, seq_count, hidden)
    piece = activated
    feed = (
        lax.psum_scatter(
            jnp.einsum("rsf,fd->rsd", piece, w_out, preferred_element_type=jnp.float32).astype(
                jnp.bfloat16
            ),
            "tensor",
            scatter_dimension=0,
            tiled=True,
        ).astype(jnp.float32)
        + b_out
    )
    output = (middle + feed).astype(jnp.bfloat16)
    positions = tensor_rank * row_count + jnp.arange(row_count, dtype=jnp.int32)
    live = positions[:, None] < seq_lengths[None, :]
    upstream = jnp.where(live[:, :, None], cotangent, jnp.zeros_like(cotangent))
    piece = lax.all_gather(upstream, "tensor", axis=0, tiled=True)
    weight_grad = jnp.einsum("rsf,rsd->fd", activated, piece, preferred_element_type=jnp.float32)
    part = jnp.einsum("rsd,fd->rsf", piece, w_out, preferred_element_type=jnp.float32)
    act_grad = part
    grad_w_out = weight_grad
    gelu_back = jax.vjp(gelu_tanh, pre_act)[1]
    pre_low = gelu_back(act_grad.reshape(seq_total * seq_count, hidden))[0].astype(jnp.bfloat16)
    grad_b_in = jnp.sum(pre_low, axis=0, dtype=jnp.float32)
    grad_w_in = jnp.einsum(
        "rd,rf->df",
        second_full.reshape(seq_total * seq_count, model_width),
        pre_low,
        preferred_element_type=jnp.float32,
    )
    pre_rows = pre_low.reshape(seq_total, seq_count, hidden)
    piece = pre_rows
    second_grad = lax.psum_scatter(
        jnp.einsum("rsf,df->rsd", piece, w_in, preferred_element_type=jnp.float32),
        "tensor",
        scatter_dimension=0,
        tiled=True,
    )
    norm_two_back = jax.vjp(layer_norm, middle, ln2_gain, ln2_bias)[1]
    middle_part, grad_ln2_gain, grad_ln2_bias = norm_two_back(second_grad)
    middle_grad = upstream.astype(jnp.float32) + middle_part
    branch_low = middle_grad.astype(jnp.bfloat16)
    grad_b_o = jnp.sum(branch_low, axis=(0, 1), dtype=jnp.float32)
    grad_b_out = jnp.sum(upstream, axis=(0, 1), dtype=jnp.float32)
    piece = lax.all_gather(branch_low, "tensor", axis=0, tiled=True)
    weight_grad = jnp.einsum("rse,rsd->ed", attended, piece, preferred_element_type=jnp.float32)
    part = jnp.einsum("rsd,ed->rse", piece, out_weight, preferred_element_type=jnp.float32)
    head_items = per_item(part.astype(jnp.bfloat16))
    grads_query, grads_keys, grads_values = lax.map(
        partial(attend_backward, block_rows=block_rows, score_scale=score_scale),
        (query_items, key_items, value_items, item_lengths, head_items, log_sums),
    )
    joint_grad = jnp.stack(
        (per_row(grads_query), per_row(grads_keys), per_row(grads_values)), axis=2
    )
    grad_b_qv = jnp.sum(joint_grad[:, :, 0::2], axis=(0, 1), dtype=jnp.float32)
    joint_rows = joint_grad.reshape(seq_total, seq_count, 3 * local_width)
    grad_w_qkv = jnp.einsum(
        "rd,rc->dc",
        normed_full.reshape(seq_total * seq_count, model_width),
        joint_rows.reshape(seq_total * seq_count, 3 * local_width),
        preferred_element_type=jnp.float32,
    )
    piece = joint_rows
    normed_grad = lax.psum_scatter(
        jnp.einsum("rsc,dc->rsd", piece, joint_weight, preferred_element_type=jnp.float32).astype(
            jnp.bfloat16
        ),
        "tensor",
        scatter_dimension=0,
        tiled=True,
    ).astype(jnp.float32)
    norm_one_back = jax.vjp(layer_norm, inputs, ln1_gain, ln1_bias)[1]
    input_part, grad_ln1_gain, grad_ln1_bias = norm_one_back(normed_grad)
    input_grad = (middle_grad + input_part).astype(jnp.bfloat16)
    summed = (
        halving_sum(grad_w_qkv.reshape(model_width, 3, local_heads, head_size) * factor, 0),
        halving_sum(weight_grad.reshape(local_heads, head_size, model_width) * factor, 2),
        halving_sum(grad_w_in * factor, 0),
        halving_sum(grad_w_out * factor, 1),
    )
    in_full = lax.dynamic_update_slice_in_dim(
        jnp.zeros((hidden * tensor_count,), jnp.float32), grad_b_in, tensor_rank * hidden, 0
    )
    joint_full = lax.dynamic_update_slice_in_dim(
        jnp.zeros((2, local_width * tensor_count), jnp.float32),
        grad_b_qv,
        tensor_rank * local_width,
        1,
    )
    shard_count = group_count * lax.axis_size("dp")
    vectors = (
        grad_ln1_gain,
        grad_ln1_bias,
        grad_b_o,
        grad_ln2_gain,
        grad_ln2_bias,
        grad_b_out,
        joint_full[0],
        joint_full[1],
        in_full,
    )
    pieces = [
        jnp.transpose((item * factor).reshape(shard_count, tensor_count, -1), (1, 0, 2))
        for item in vectors
    ]
    widths = [piece.shape[2] for piece in pieces]
    packed = jnp.concatenate(pieces, 2)
    packed = halving_steps(
        packed,
        0,
        [
            ("tensor", tensor_count, 8),
            ("tensor", tensor_count, 4),
            ("tensor", tensor_count, 2),
            ("tensor", tensor_count, 1),
        ],
    )
    packed = halving_steps(
        packed,
        1,
        [("group", group_count, 2), ("group", group_count, 1), ("dp", lax.axis_size("dp"), 1)],
    )
    flat = packed.reshape(-1)
    parts = []
    offset = 0
    for width in widths:
        parts.append(flat[offset : offset + width])
        offset += width
    return (
        output,
        input_grad,
        parts[0],
        parts[1],
        summed[0],
        jnp.stack((parts[6], parts[7])),
        summed[1],
        parts[2],
        parts[3],
        parts[4],
        summed[2],
        parts[8],
        summed[3],
        parts[5],
    )


def halving_steps(value, dim, steps, send_type=None):
    for axis, size, bit in steps:
        half = value.shape[dim] // 2
        low_half = lax.slice_in_dim(value, 0, half, axis=dim)
        high_half = lax.slice_in_dim(value, half, 2 * half, axis=dim)
        upper = lax.axis_index(axis) // bit % 2 == 1
        keep = jnp.where(upper, high_half, low_half)
        send = jnp.where(upper, low_half, high_half)
        if send_type is not None:
            send = send.astype(send_type)
        got = lax.ppermute(send, axis, [(i, i ^ bit) for i in range(size)])
        value = keep + got.astype(keep.dtype)
    return value


def halving_sum(value, dim):
    shape = value.shape
    groups = lax.axis_size("group")
    dps = lax.axis_size("dp")
    split = shape[:dim] + (groups * dps, shape[dim] // (groups * dps)) + shape[dim + 1 :]
    value = value.reshape(split)
    value = halving_steps(
        value, dim, [("group", groups, 2), ("group", groups, 1), ("dp", dps, 1)], jnp.bfloat16
    )
    return value.reshape(shape[:dim] + (shape[dim] // (groups * dps),) + shape[dim + 1 :])


def solution(mesh):
    in_specs = (
        P("tensor", ("group", "dp"), None),
        P("tensor", ("group", "dp"), None),
        P(),
        P(),
        P(),
        P(None, None, "tensor", None),
        P(None, "tensor"),
        P("tensor", None, None),
        P(),
        P(),
        P(),
        P(None, "tensor"),
        P("tensor"),
        P("tensor", None),
        P(),
    )
    out_specs = (
        P("tensor", ("group", "dp"), None),
        P("tensor", ("group", "dp"), None),
        P(("group", "dp", "tensor")),
        P(("group", "dp", "tensor")),
        P(("group", "dp"), None, "tensor", None),
        P(None, ("group", "dp", "tensor")),
        P("tensor", None, ("group", "dp")),
        P(("group", "dp", "tensor")),
        P(("group", "dp", "tensor")),
        P(("group", "dp", "tensor")),
        P(("group", "dp"), "tensor"),
        P(("group", "dp", "tensor")),
        P("tensor", ("group", "dp")),
        P(("group", "dp", "tensor")),
    )
    return jax.shard_map(shards, mesh=mesh, in_specs=in_specs, out_specs=out_specs, check_vma=False)
```

profile of v0, /device:TPU:0, one launch (start us, length us, event | category | flops | bytes accessed | tf_op | source)
XLA Modules:
  0.0 947.7 jit_solution(5569445801283736321)
XLA Ops:
  12.8 2.7 copy.44
  16.8 69.2 %all-gather.5.cloned.1.call-done = bf16[2048,1,2048]{2,0,1:T(8,128)(2,1)} async-done(((bf16[128,1,2048]{2,0,1:T(8,128)(2,1)}), bf16[2048,1,2048]{2,0,1:T(8,128)(2,1)}) %all-gather.5.cloned.1.call-update) | async-done | bytes 8388624 | tf_op jit(solution)/shard_map/all_gather | solution.py:132
  86.0 7.4 fusion.33
  94.7 2.9 fusion.119
  97.7 3.3 fusion.122
  101.0 4.0 online-softmax.3
  106.0 4.6 fusion.121
  110.6 4.0 online-softmax.2
  115.5 4.6 fusion.120
  120.1 4.0 online-softmax.1
  125.2 4.2 online-softmax
  130.4 8.1 convolution_bitcast_fusion.1
  138.6 110.4 %reduce-scatter.5.cloned.1.call-done = f32[128,1,2048]{2,0,1:T(8,128)} async-done(((f32[2048,1,2048]{2,0,1:T(8,128)}), f32[128,1,2048]{2,0,1:T(8,128)}) %reduce-scatter.5.cloned.1.call-update) | async-done | bytes 1048592 | tf_op jit(solution)/shard_map/reduce_scatter | solution.py:166
  254.8 67.5 %all-gather.7.cloned.1.call-done = bf16[2048,1,2048]{2,0,1:T(8,128)(2,1)} async-done(((bf16[128,1,2048]{2,0,1:T(8,128)(2,1)}), bf16[2048,1,2048]{2,0,1:T(8,128)(2,1)}) %all-gather.7.cloned.1.call-update) | async-done | bytes 8388624 | tf_op jit(solution)/shard_map/all_gather | solution.py:176
  322.3 10.5 %fusion.10 = f32[2048,512]{1,0:T(8,128)} fusion(bf16[2048,512]{1,0:T(8,128)(2,1)} %param.26, bf16[2048,1,2048]{2,0,1:T(8,128)(2,1)} %all-gather.7.cloned.1.call-done), kind=kOutput, calls=%fused_computation.12 | convolution fusion | flops 4294967296 | bytes 14680064 | tf_op jit(solution)/shard_map/dot_general | solution.py:178
  332.8 62.4 %all-gather.9.cloned.1.call-done = bf16[2048,1,2048]{2,0,1:T(8,128)(2,1)} async-done(((bf16[128,1,2048]{2,0,1:T(8,128)(2,1)}), bf16[2048,1,2048]{2,0,1:T(8,128)(2,1)}) %all-gather.9.cloned.1.call-update) | async-done | bytes 8388624 | tf_op jit(solution)/shard_map/all_gather | solution.py:202
  395.2 12.7 %convert_reduce_fusion = (f32[512]{0:T(512)}, bf16[2048,512]{1,0:T(8,128)(2,1)S(1)}) fusion(f32[2048,512]{1,0:T(8,128)} %fusion.10, f32[512]{0:T(512)S(1)} %copy-done.72, bf16[512,2048]{1,0:T(8,128)(2,1)S(1)} %copy-done, bf16[2048,1,2048]{2,0,1:T(8,128)(2,1)} %all-gather.9.cloned.1.call-done), kind=kOutput, calls=%fused_computation.29 | convolution fusion | flops 4319084032 | bytes 16781312 | tf_op jit(solution)/shard_map/rsd,fd->rsf/dot_general | solution.py:204
  409.3 8.3 convolution_bitcast_fusion
  417.7 10.2 %convert_bitcast_fusion.1 = bf16[2048,1,2048]{2,0,1:T(8,128)(2,1)} fusion(bf16[512,2048]{1,0:T(8,128)(2,1)S(1)} %copy-done, f32[2048,512]{1,0:T(8,128)} %fusion.10, f32[512]{0:T(512)S(1)} %copy-done.72), kind=kOutput, calls=%fused_computation.19 | convolution fusion | flops 4309647360 | bytes 14682112 | tf_op jit(solution)/shard_map/rsf,fd->rsd/dot_general | solution.py:189
  428.0 100.0 %reduce-scatter.9.cloned.1.call-done = f32[128,1,2048]{2,0,1:T(8,128)} async-done(((f32[2048,1,2048]{2,0,1:T(8,128)}), f32[128,1,2048]{2,0,1:T(8,128)}) %reduce-scatter.9.cloned.1.call-update) | async-done | bytes 1048592 | tf_op jit(solution)/shard_map/reduce_scatter | solution.py:218
  530.2 85.8 %reduce-scatter.7.cloned.1.call-done = bf16[128,1,2048]{2,0,1:T(8,128)(2,1)} async-done(((bf16[2048,1,2048]{2,0,1:T(8,128)(2,1)}), bf16[128,1,2048]{2,0,1:T(8,128)(2,1)}) %reduce-scatter.7.cloned.1.call-update) | async-done | bytes 524304 | tf_op jit(solution)/shard_map/reduce_scatter | solution.py:188
  616.0 2.6 fusion.115
  619.9 3.0 exponential_reduce_fusion
  628.1 61.8 %all-gather.11.cloned.1.call-done = bf16[2048,1,2048]{2,0,1:T(8,128)(2,1)} async-done(((bf16[128,1,2048]{2,0,1:T(8,128)(2,1)}), bf16[2048,1,2048]{2,0,1:T(8,128)(2,1)}) %all-gather.11.cloned.1.call-update) | async-done | bytes 8388624 | tf_op jit(solution)/shard_map/all_gather | solution.py:230
  689.9 5.7 fusion.45
  695.6 2.7 fusion.96
  698.4 2.8 fusion.99
  701.2 2.8 fusion.102
  707.7 10.2 %multiply_reduce_fusion = (f32[512]{0:T(512)}, f32[512]{0:T(512)}, f32[512]{0:T(512)}, f32[512]{0:T(512)}, f32[512,2048]{1,0:T(8,128)}) fusion(f32[512,2048]{1,0:T(8,128)S(1)} %copy-done.2, f32[512]{0:T(512)S(1)} %get-tuple-element.117, pred[2048]{0:T(1024)(128)(4,1)S(1)} %iota_compare_fusion.4, s32[512]{0:T(512)S(1)} %iota_add_fusion, ...), kind=kOutput, calls=%fused_computation.31 | convolution fusion | flops 293599232 | bytes 34234368 | tf_op jit(solution)/shard_map/while/body/eval_jaxpr/dot_general | solution.py:65
  717.9 9.4 multiply_convert_fusion
  744.5 9.7 %convert_bitcast_fusion = bf16[2048,1,2048]{2,0,1:T(8,128)(2,1)} fusion(bf16[2048,384]{0,1:T(8,128)(2,1)} %bitcast.201, bf16[2048,384]{0,1:T(8,128)(2,1)} %bitcast.202), kind=kOutput, calls=%fused_computation.18 | convolution fusion | flops 3225419776 | bytes 11534336 | tf_op jit(solution)/shard_map/rsc,dc->rsd/dot_general | solution.py:251
  757.6 8.7 fusion.27
  768.3 7.1 fusion.30
  783.2 2.8 slice_select_fusion
  786.0 17.0 %collective-permute-done.13 = bf16[4,256,512]{2,1,0:T(8,128)(2,1)S(1)} collective-permute-done((bf16[4,256,512]{2,1,0:T(8,128)(2,1)}, bf16[4,256,512]{2,1,0:T(8,128)(2,1)S(1)}, u32[]{:S(2)}, u32[]{:S(2)}) %collective-permute-start.13) | collective-permute-done | bytes 1048608 | tf_op jit(solution)/shard_map/ppermute | solution.py:343
  803.6 20.9 %collective-permute-done.16 = bf16[512,4,256]{2,0,1:T(8,128)(2,1)} collective-permute-done((bf16[512,4,256]{2,0,1:T(8,128)(2,1)}, bf16[512,4,256]{2,0,1:T(8,128)(2,1)}, u32[]{:S(2)}, u32[]{:S(2)}) %collective-permute-start.16) | collective-permute-done | bytes 1048608 | tf_op jit(solution)/shard_map/ppermute | solution.py:343
  827.0 3.2 collective-permute-start.15
  834.3 3.4 collective-permute-done.15
  838.6 4.3 collective-permute-done.18
  846.7 4.7 fusion.42
  853.7 7.0 fusion.36
  864.6 2.9 collective-permute-start.12
  877.2 3.2 collective-permute-start
  880.4 25.4 %collective-permute-done.7 = bf16[4,256,3,1,128]{4,3,2,1,0:T(2,128)(2,1)} collective-permute-done((bf16[4,256,3,1,128]{4,3,2,1,0:T(2,128)(2,1)S(1)}, bf16[4,256,3,1,128]{4,3,2,1,0:T(2,128)(2,1)}, u32[]{:S(2)}, u32[]{:S(2)}) %collective-permute-start.7) | collective-permute-done | bytes 786464 | tf_op jit(solution)/shard_map/ppermute | solution.py:343
  905.8 4.3 copy_add_fusion
  914.3 3.0 collective-permute-start.2
  923.8 7.1 collective-permute-done.9
  935.7 3.1 collective-permute-done.6
  (325 shorter events, 104.7 us)
Async XLA Ops:
  7.2 388.0 %copy-start = (bf16[512,2048]{1,0:T(8,128)(2,1)S(1)}, bf16[512,2048]{1,0:T(8,128)(2,1)}, u32[]{:S(2)}) copy-start(bf16[512,2048]{1,0:T(8,128)(2,1)} %param.28) | copy-start | bytes 6291460
  7.2 78.8 %all-gather.5.cloned.1.call-start = ((), (), s32[]{:S(2)}) async-start(), calls=%async_computation.4 | async-start | bytes 8912896 | tf_op jit(solution)/shard_map/all_gather | solution.py:132
  9.9 83.5 %copy-start.70 = (f32[128]{0:T(128)}, f32[128]{0:T(128)S(1)}, u32[]{:S(2)}) copy-start(f32[128]{0:T(128)S(1)} %fusion.75) | copy-start | bytes 1540
  12.8 236.2 %reduce-scatter.5.cloned.1.call-start = ((), (), s32[]{:S(2)}) async-start(), calls=%async_computation.5 | async-start | bytes 17825792 | tf_op jit(solution)/shard_map/reduce_scatter | solution.py:166
  16.1 689.9 %copy-start.47 = (s32[512]{0:T(512)}, s32[512]{0:T(512)S(1)}, u32[]{:S(2)}) copy-start(s32[512]{0:T(512)S(1)} %iota_add_fusion.2) | copy-start | bytes 6148
  16.1 689.9 %copy-start.45 = (s32[512]{0:T(512)}, s32[512]{0:T(512)S(1)}, u32[]{:S(2)}) copy-start(s32[512]{0:T(512)S(1)} %iota_add_fusion) | copy-start | bytes 6148
  106.0 24.4 %copy-start.27 = (bf16[512,128]{1,0:T(8,128)(2,1)}, bf16[512,128]{1,0:T(8,128)(2,1)S(1)}, u32[]{:S(2)}) copy-start(bf16[512,128]{1,0:T(8,128)(2,1)S(1)} %convert_element_type.280) | copy-start | bytes 393220
  138.5 110.5 %copy-start.58 = (f32[2048]{0:T(1024)S(1)}, f32[2048]{0:T(1024)}, u32[]{:S(2)}) copy-start(f32[2048]{0:T(1024)} %param.23) | copy-start | bytes 24580
  138.5 112.3 %copy-start.43 = (f32[2048]{0:T(1024)S(1)}, f32[2048]{0:T(1024)}, u32[]{:S(2)}) copy-start(f32[2048]{0:T(1024)} %param.24) | copy-start | bytes 24580
  138.5 112.3 %copy-start.59 = (f32[2048]{0:T(1024)S(1)}, f32[2048]{0:T(1024)}, u32[]{:S(2)}) copy-start(f32[2048]{0:T(1024)} %param.25) | copy-start | bytes 24580
  138.6 183.7 %all-gather.7.cloned.1.call-start = ((), (), s32[]{:S(2)}) async-start(), calls=%async_computation.6 | async-start | bytes 8912896 | tf_op jit(solution)/shard_map/all_gather | solution.py:176
  251.9 143.3 %all-gather.9.cloned.1.call-start = ((), (), s32[]{:S(2)}) async-start(), calls=%async_computation.8 | async-start | bytes 8912896 | tf_op jit(solution)/shard_map/all_gather | solution.py:202
  254.7 140.5 %copy-start.72 = (f32[512]{0:T(512)S(1)}, f32[512]{0:T(512)}, u32[]{:S(2)}) copy-start(f32[512]{0:T(512)} %param.27) | copy-start | bytes 6148
  254.7 273.3 %reduce-scatter.9.cloned.1.call-start = ((), (), s32[]{:S(2)}) async-start(), calls=%async_computation.9 | async-start | bytes 17825792 | tf_op jit(solution)/shard_map/reduce_scatter | solution.py:218
  417.6 198.4 %reduce-scatter.7.cloned.1.call-start = ((), (), s32[]{:S(2)}) async-start(), calls=%async_computation.7 | async-start | bytes 8912896 | tf_op jit(solution)/shard_map/reduce_scatter | solution.py:188
  427.9 188.1 %copy-start.60 = (f32[2048]{0:T(1024)S(1)}, f32[2048]{0:T(1024)}, u32[]{:S(2)}) copy-start(f32[2048]{0:T(1024)} %param.29) | copy-start | bytes 24580
  427.9 190.6 %copy-start.21 = (bf16[128,1,2048]{2,0,1:T(8,128)(2,1)S(1)}, bf16[128,1,2048]{2,0,1:T(8,128)(2,1)}, u32[]{:S(2)}) copy-start(bf16[128,1,2048]{2,0,1:T(8,128)(2,1)} %get-tuple-element.79) | copy-start | bytes 1572868
  427.9 261.9 %all-gather.11.cloned.1.call-start = ((), (), s32[]{:S(2)}) async-start(), calls=%async_computation.10 | async-start | bytes 8912896 | tf_op jit(solution)/shard_map/all_gather | solution.py:230
  619.7 252.5 %reduce-scatter.11.cloned.1.call-start = ((), (), s32[]{:S(2)}) async-start(), calls=%async_computation.11 | async-start | bytes 8912896 | tf_op jit(solution)/shard_map/reduce_scatter | solution.py:250
  624.1 81.8 %copy-start.49 = (f32[512]{0:T(512)}, f32[512]{0:T(512)S(1)}, u32[]{:S(2)}) copy-start(f32[512]{0:T(512)S(1)} %get-tuple-element.118) | copy-start | bytes 6148
  624.1 81.8 %copy-start.51 = (f32[512]{0:T(512)}, f32[512]{0:T(512)S(1)}, u32[]{:S(2)}) copy-start(f32[512]{0:T(512)S(1)} %get-tuple-element.117) | copy-start | bytes 6148
  624.6 65.3 %copy-start.38 = (bf16[1,128,2048]{2,1,0:T(8,128)(2,1)S(1)}, bf16[1,128,2048]{2,1,0:T(8,128)(2,1)}, u32[]{:S(2)}) copy-start(bf16[1,128,2048]{2,1,0:T(8,128)(2,1)} %param.22) | copy-start | bytes 1572868
  626.8 79.2 %copy-start.53 = (f32[512]{0:T(512)}, f32[512]{0:T(512)S(1)}, u32[]{:S(2)}) copy-start(f32[512]{0:T(512)S(1)} %get-tuple-element.119) | copy-start | bytes 6148
  626.8 79.2 %copy-start.55 = (f32[512]{0:T(512)}, f32[512]{0:T(512)S(1)}, u32[]{:S(2)}) copy-start(f32[512]{0:T(512)S(1)} %get-tuple-element.120) | copy-start | bytes 6148
  776.8 26.3 %collective-permute-start.13 = (bf16[4,256,512]{2,1,0:T(8,128)(2,1)}, bf16[4,256,512]{2,1,0:T(8,128)(2,1)S(1)}, u32[]{:S(2)}, u32[]{:S(2)}) collective-permute-start(bf16[4,256,512]{2,1,0:T(8,128)(2,1)} %bitcast.57), channel_id=1, source_target_pairs={{0,64},{32,96},{64,0},{96,32},{1,65},{33,97},{65,1},{97,33},{2,66}... | collective-permute-start | bytes 3145736 | tf_op jit(solution)/shard_map/ppermute | solution.py:343
  781.9 42.6 %collective-permute-start.16 = (bf16[512,4,256]{2,0,1:T(8,128)(2,1)}, bf16[512,4,256]{2,0,1:T(8,128)(2,1)}, u32[]{:S(2)}, u32[]{:S(2)}) collective-permute-start(bf16[512,4,256]{2,0,1:T(8,128)(2,1)} %select_convert_fusion), channel_id=1, source_target_pairs={{0,64},{32,96},{64,0},{96,32},{1,65},{33,97},{65,1},{97,33},{2,66}... | collective-permute-start | bytes 3145736 | tf_op jit(solution)/shard_map/ppermute | solution.py:343
  786.0 38.4 %copy-start.13 = (f32[512,4,256]{2,1,0:T(4,128)S(1)}, f32[512,4,256]{2,1,0:T(4,128)}, u32[]{:S(2)}) copy-start(f32[512,4,256]{2,1,0:T(4,128)} %copy-done.12) | copy-start | bytes 6291460
  803.5 23.1 %collective-permute-start.14 = (bf16[2,256,512]{2,1,0:T(8,128)(2,1)S(1)}, bf16[2,256,512]{2,1,0:T(8,128)(2,1)S(1)}, u32[]{:S(2)}, u32[]{:S(2)}) collective-permute-start(bf16[2,256,512]{2,1,0:T(8,128)(2,1)S(1)} %select_convert_fusion.4), channel_id=1, source_target_pairs={{0,32},{32,0},{64,96},{96,64},{1,33},{33,1},{65,97},{97,65},{2,34}... | collective-permute-start | bytes 1572872 | tf_op jit(solution)/shard_map/ppermute | solution.py:343
  826.5 3.7 collective-permute-start.17
  827.0 10.7 %collective-permute-start.15 = (bf16[1,256,512]{2,1,0:T(8,128)(2,1)S(1)}, bf16[1,256,512]{2,1,0:T(8,128)(2,1)S(1)}, u32[]{:S(2)}, u32[]{:S(2)}) collective-permute-start(bf16[1,256,512]{2,1,0:T(8,128)(2,1)S(1)} %select_convert_fusion.6), channel_id=1, source_target_pairs={{0,16},{16,0},{1,17},{17,1},{2,18},{18,2},{3,19},{19,3},{4,20},{20... | collective-permute-start | bytes 786440 | tf_op jit(solution)/shard_map/ppermute | solution.py:343
  831.2 11.7 %collective-permute-start.18 = (bf16[512,1,256]{2,0,1:T(8,128)(2,1)}, bf16[512,1,256]{2,0,1:T(8,128)(2,1)S(1)}, u32[]{:S(2)}, u32[]{:S(2)}) collective-permute-start(bf16[512,1,256]{2,0,1:T(8,128)(2,1)} %select_convert_fusion.5), channel_id=1, source_target_pairs={{0,16},{16,0},{1,17},{17,1},{2,18},{18,2},{3,19},{19,3},{4,20},{20... | collective-permute-start | bytes 786440 | tf_op jit(solution)/shard_map/ppermute | solution.py:343
  852.0 10.2 %collective-permute-start.10 = (bf16[1,128,4,256]{3,1,2,0:T(8,128)(2,1)S(1)}, bf16[1,128,4,256]{3,1,2,0:T(8,128)(2,1)S(1)}, u32[]{:S(2)}, u32[]{:S(2)}) collective-permute-start(bf16[1,128,4,256]{3,1,2,0:T(8,128)(2,1)S(1)} %select_convert_fusion.7), channel_id=1, source_target_pairs={{0,64},{32,96},{64,0},{96,32},{1,65},{33,97},{65,1},{97,33},{2,66}... | collective-permute-start | bytes 786440 | tf_op jit(solution)/shard_map/ppermute | solution.py:343
  862.4 1.4 collective-permute-start.11
  864.6 6.1 collective-permute-start.12
  869.5 36.4 %collective-permute-start.7 = (bf16[4,256,3,1,128]{4,3,2,1,0:T(2,128)(2,1)S(1)}, bf16[4,256,3,1,128]{4,3,2,1,0:T(2,128)(2,1)}, u32[]{:S(2)}, u32[]{:S(2)}) collective-permute-start(bf16[4,256,3,1,128]{4,3,2,1,0:T(2,128)(2,1)S(1)} %copy.55), channel_id=1, source_target_pairs={{0,64},{32,96},{64,0},{96,32},{1,65},{33,97},{65,1},{97,33},{2,66}... | collective-permute-start | bytes 2359304 | tf_op jit(solution)/shard_map/ppermute | solution.py:343
  877.2 33.0 %collective-permute-start = (f32[8,8,192]{2,0,1:T(8,128)S(1)}, f32[8,8,192]{2,0,1:T(8,128)S(1)}, u32[]{:S(2)}, u32[]{:S(2)}) collective-permute-start(f32[8,8,192]{2,0,1:T(8,128)S(1)} %slice_select_fusion.2), channel_id=1, source_target_pairs={{0,8},{1,9},{2,10},{3,11},{4,12},{5,13},{6,14},{7,15},{8,0},{9,1},... | collective-permute-start | bytes 147464 | tf_op jit(solution)/shard_map/ppermute | solution.py:343
  910.2 24.2 %copy-start.20 = (f32[128,1,2048]{2,0,1:T(8,128)S(1)}, f32[128,1,2048]{2,0,1:T(8,128)}, u32[]{:S(2)}) copy-start(f32[128,1,2048]{2,0,1:T(8,128)} %copy-done.19) | copy-start | bytes 3145732
  910.2 24.2 %copy-start.22 = (bf16[128,1,2048]{2,0,1:T(8,128)(2,1)S(1)}, bf16[128,1,2048]{2,0,1:T(8,128)(2,1)}, u32[]{:S(2)}) copy-start(bf16[128,1,2048]{2,0,1:T(8,128)(2,1)} %get-tuple-element.79) | copy-start | bytes 1572868
  910.2 24.2 %copy-start.23 = (bf16[128,1,2048]{2,0,1:T(8,128)(2,1)S(1)}, bf16[128,1,2048]{2,0,1:T(8,128)(2,1)}, u32[]{:S(2)}) copy-start(bf16[128,1,2048]{2,0,1:T(8,128)(2,1)} %reduce-scatter.11.cloned.1.call-done) | copy-start | bytes 1572868
  910.2 4.0 collective-permute-start.1
  912.5 4.8 collective-permute-start.8
  914.2 26.2 %copy-start.1 = (bf16[512,2048]{1,0:T(8,128)(2,1)S(1)}, bf16[512,2048]{1,0:T(8,128)(2,1)}, u32[]{:S(2)}) copy-start(bf16[512,2048]{1,0:T(8,128)(2,1)} %param.28) | copy-start | bytes 6291460
  914.3 5.3 collective-permute-start.2
  919.6 3.7 collective-permute-start.3
  921.5 9.4 collective-permute-start.9
  923.4 8.9 collective-permute-start.4
  932.4 1.2 collective-permute-start.5
  933.6 5.2 collective-permute-start.6
  (56 other events, 428.1 us)
Sparse Core Ops, SparseCore 0:
  12.9 73.0 all-gather.4
  138.7 110.2 reduce-scatter.4
  252.1 70.1 all-gather.6
  324.8 70.3 all-gather.8
  417.7 110.1 reduce-scatter.8
  531.2 84.7 reduce-scatter.6
  619.8 70.0 all-gather.10
  754.4 84.8 reduce-scatter.10
where the time goes:
time: 957 us; the launch traced here: 948 us
  waiting for transfers between devices  645 us (67%)
  matrix products  149 us (16%)
  other arithmetic  72.5 us (8%)
  starting transfers between devices  24.1 us (3%)
  local copies, waits for them, and re-layouts  24 us (3%)
  between operations  17.3 us (2%)
  Pallas kernels  16.2 us (2%)
    reduce_scatter x1, waiting for transfers between devices, shards(): lax.psum_scatter(jnp.einsum('rse,ed->rsd', piece, out_weight, preferred_e...  110 us
    reduce_scatter x1, waiting for transfers between devices, shards(): lax.psum_scatter(jnp.einsum('rsf,df->rsd', piece, w_in, preferred_element...  100 us
    ppermute x19, waiting for transfers between devices, halving_steps(): got = lax.ppermute(send, axis, [(i, i ^ bit) for i in range(size)])  87.8 us
    reduce_scatter x1, waiting for transfers between devices, shards(): lax.psum_scatter(jnp.einsum('rsf,fd->rsd', piece, w_out, preferred_elemen...  85.8 us
    all_gather x1, waiting for transfers between devices, shards(): normed_full = lax.all_gather(normed_low, 'tensor', axis=0, tiled=True)  69.2 us
    all_gather x1, waiting for transfers between devices, shards(): second_full = lax.all_gather(second_low, 'tensor', axis=0, tiled=True)  67.5 us
    all_gather x1, waiting for transfers between devices, shards(): piece = lax.all_gather(upstream, 'tensor', axis=0, tiled=True)  62.4 us
    all_gather x1, waiting for transfers between devices, shards(): piece = lax.all_gather(branch_low, 'tensor', axis=0, tiled=True)  61.8 us
  transfers between devices with their start and end apart: 27, of which 20 were waited for; matrix products, arithmetic and copies ran while one was open for 11% of the time, Pallas kernels for 0%

commit v1 on v0

--- a/solution.py
+++ b/solution.py
@@ -129,7 +129,9 @@
     )
     inputs = tokens.astype(jnp.float32)
     normed_low = layer_norm(inputs, ln1_gain, ln1_bias).astype(jnp.bfloat16)
-    normed_full = lax.all_gather(normed_low, "tensor", axis=0, tiled=True)
+    normed_full = jnp.concatenate(
+        lax.all_to_all(jnp.stack([normed_low] * lax.axis_size("tensor")), "tensor", 0, 0), axis=0
+    )
     joint_weight = w_qkv.reshape(model_width, 3 * local_width)
     projected = jnp.dot(
         normed_full.reshape(seq_total * seq_count, model_width),

time: 957 us -> 1050 us (1.097)
  waiting for transfers between devices: 645 us -> 723 us
    all_to_all x0 -> x1, waiting for transfers between devices: none -> 144 us  [shards(): lax.all_to_all(jnp.stack([normed_low] * lax.axis_size('tensor')), 'tensor...]
    all_gather x1 -> x0, waiting for transfers between devices: 69.2 us -> none  [shards(): normed_full = lax.all_gather(normed_low, 'tensor', axis=0, tiled=True)]
  transfers between devices with their start and end apart: 27 -> 27, of which waited for: 20 -> 20; matrix products, arithmetic and copies ran while one was open for 11% -> 10% of each run, Pallas kernels for 0% -> 0%
where the time goes in v1:
time: 1050 us; the launch traced here: 1040 us
  waiting for transfers between devices  723 us (69%)
  matrix products  149 us (14%)
  other arithmetic  71.7 us (7%)
  starting transfers between devices  31.5 us (3%)
  local copies, waits for them, and re-layouts  28.8 us (3%)
  between operations  17.2 us (2%)
  Pallas kernels  16.2 us (2%)
    all_to_all x1, waiting for transfers between devices, shards(): lax.all_to_all(jnp.stack([normed_low] * lax.axis_size('tensor')), 'tensor...  144 us
    reduce_scatter x1, waiting for transfers between devices, shards(): lax.psum_scatter(jnp.einsum('rse,ed->rsd', piece, out_weight, preferred_e...  114 us
    reduce_scatter x1, waiting for transfers between devices, shards(): lax.psum_scatter(jnp.einsum('rsf,df->rsd', piece, w_in, preferred_element...  100 us
    ppermute x19, waiting for transfers between devices, halving_steps(): got = lax.ppermute(send, axis, [(i, i ^ bit) for i in range(size)])  87.7 us
    reduce_scatter x1, waiting for transfers between devices, shards(): lax.psum_scatter(jnp.einsum('rsf,fd->rsd', piece, w_out, preferred_elemen...  85.6 us
    all_gather x1, waiting for transfers between devices, shards(): second_full = lax.all_gather(second_low, 'tensor', axis=0, tiled=True)  67.6 us
    all_gather x1, waiting for transfers between devices, shards(): piece = lax.all_gather(upstream, 'tensor', axis=0, tiled=True)  62.5 us
    all_gather x1, waiting for transfers between devices, shards(): piece = lax.all_gather(branch_low, 'tensor', axis=0, tiled=True)  61.8 us
  transfers between devices with their start and end apart: 27, of which 20 were waited for; matrix products, arithmetic and copies ran while one was open for 10% of the time, Pallas kernels for 0%

profile of v1, /device:TPU:0, one launch (start us, length us, event | category | flops | bytes accessed | tf_op | source)
XLA Modules:
  0.0 1037.3 jit_solution(14607841363049635191)
XLA Ops:
  12.4 4.3 stack.10
  16.7 7.3 all-to-all-start
  28.0 143.7 %all-to-all-done = bf16[16,128,1,2048]{3,1,2,0:T(8,128)(2,1)} async-done(((bf16[16,128,1,2048]{3,1,2,0:T(8,128)(2,1)}), bf16[16,128,1,2048]{3,1,2,0:T(8,128)(2,1)}, u32[]{:S(2)}, u32[]{:S(2)}) %all-to-all-start) | async-done | bytes 8388640 | tf_op jit(solution)/shard_map/all_to_all | solution.py:133
  171.7 7.4 convolution_bitcast_fusion.2
  180.4 2.9 fusion.110
  183.4 3.3 fusion.113
  186.7 4.0 online-softmax.3
  191.7 4.6 fusion.112
  196.3 4.0 online-softmax.2
  201.2 4.6 fusion.111
  205.9 4.0 online-softmax.1
  210.9 4.2 online-softmax
  216.1 8.1 convolution_bitcast_fusion.1
  224.3 114.3 %reduce-scatter.5.cloned.1.call-done = f32[128,1,2048]{2,0,1:T(8,128)} async-done(((f32[2048,1,2048]{2,0,1:T(8,128)}), f32[128,1,2048]{2,0,1:T(8,128)}) %reduce-scatter.5.cloned.1.call-update) | async-done | bytes 1048592 | tf_op jit(solution)/shard_map/reduce_scatter | solution.py:168
  344.4 67.6 %all-gather.4.cloned.1.call-done = bf16[2048,1,2048]{2,0,1:T(8,128)(2,1)} async-done(((bf16[128,1,2048]{2,0,1:T(8,128)(2,1)}), bf16[2048,1,2048]{2,0,1:T(8,128)(2,1)}) %all-gather.4.cloned.1.call-update) | async-done | bytes 8388624 | tf_op jit(solution)/shard_map/all_gather | solution.py:178
  411.9 10.6 %fusion.10 = f32[2048,512]{1,0:T(8,128)} fusion(bf16[2048,512]{1,0:T(8,128)(2,1)} %param.26, bf16[2048,1,2048]{2,0,1:T(8,128)(2,1)} %all-gather.4.cloned.1.call-done), kind=kOutput, calls=%fused_computation.12 | convolution fusion | flops 4294967296 | bytes 14680064 | tf_op jit(solution)/shard_map/dot_general | solution.py:180
  422.5 62.5 %all-gather.6.cloned.1.call-done = bf16[2048,1,2048]{2,0,1:T(8,128)(2,1)} async-done(((bf16[128,1,2048]{2,0,1:T(8,128)(2,1)}), bf16[2048,1,2048]{2,0,1:T(8,128)(2,1)}) %all-gather.6.cloned.1.call-update) | async-done | bytes 8388624 | tf_op jit(solution)/shard_map/all_gather | solution.py:204
  485.0 12.7 %convert_reduce_fusion = (f32[512]{0:T(512)}, bf16[2048,512]{1,0:T(8,128)(2,1)S(1)}) fusion(f32[2048,512]{1,0:T(8,128)} %fusion.10, f32[512]{0:T(512)S(1)} %copy-done.72, bf16[512,2048]{1,0:T(8,128)(2,1)S(1)} %copy-done, bf16[2048,1,2048]{2,0,1:T(8,128)(2,1)} %all-gather.6.cloned.1.call-done), kind=kOutput, calls=%fused_computation.25 | convolution fusion | flops 4319084032 | bytes 16781312 | tf_op jit(solution)/shard_map/rsd,fd->rsf/dot_general | solution.py:206
  499.1 8.2 convolution_bitcast_fusion
  507.3 10.2 convert_bitcast_fusion.1
  517.7 100.0 %reduce-scatter.9.cloned.1.call-done = f32[128,1,2048]{2,0,1:T(8,128)} async-done(((f32[2048,1,2048]{2,0,1:T(8,128)}), f32[128,1,2048]{2,0,1:T(8,128)}) %reduce-scatter.9.cloned.1.call-update) | async-done | bytes 1048592 | tf_op jit(solution)/shard_map/reduce_scatter | solution.py:220
  620.0 85.6 %reduce-scatter.7.cloned.1.call-done = bf16[128,1,2048]{2,0,1:T(8,128)(2,1)} async-done(((bf16[2048,1,2048]{2,0,1:T(8,128)(2,1)}), bf16[128,1,2048]{2,0,1:T(8,128)(2,1)}) %reduce-scatter.7.cloned.1.call-update) | async-done | bytes 524304 | tf_op jit(solution)/shard_map/reduce_scatter | solution.py:190
  709.5 3.0 exponential_reduce_fusion
  717.7 61.8 %all-gather.8.cloned.1.call-done = bf16[2048,1,2048]{2,0,1:T(8,128)(2,1)} async-done(((bf16[128,1,2048]{2,0,1:T(8,128)(2,1)}), bf16[2048,1,2048]{2,0,1:T(8,128)(2,1)}) %all-gather.8.cloned.1.call-update) | async-done | bytes 8388624 | tf_op jit(solution)/shard_map/all_gather | solution.py:232
  779.4 5.7 fusion.35
  785.2 2.7 fusion.87
  787.9 2.8 fusion.90
  790.7 2.8 fusion.93
  797.2 10.2 multiply_reduce_fusion
  807.4 9.4 multiply_convert_fusion
  834.1 9.7 convert_bitcast_fusion
  847.2 8.7 fusion.23
  857.9 7.1 fusion.26
  872.8 2.8 slice_select_fusion
  875.6 17.0 %collective-permute-done.13 = bf16[4,256,512]{2,1,0:T(8,128)(2,1)S(1)} collective-permute-done((bf16[4,256,512]{2,1,0:T(8,128)(2,1)}, bf16[4,256,512]{2,1,0:T(8,128)(2,1)S(1)}, u32[]{:S(2)}, u32[]{:S(2)}) %collective-permute-start.13) | collective-permute-done | bytes 1048608 | tf_op jit(solution)/shard_map/ppermute | solution.py:345
  893.1 20.9 %collective-permute-done.16 = bf16[512,4,256]{2,0,1:T(8,128)(2,1)} collective-permute-done((bf16[512,4,256]{2,0,1:T(8,128)(2,1)}, bf16[512,4,256]{2,0,1:T(8,128)(2,1)}, u32[]{:S(2)}, u32[]{:S(2)}) %collective-permute-start.16) | collective-permute-done | bytes 1048608 | tf_op jit(solution)/shard_map/ppermute | solution.py:345
  916.5 3.2 collective-permute-start.15
  923.8 3.4 collective-permute-done.15
  928.2 4.3 collective-permute-done.18
  936.2 4.7 fusion.32
  943.2 7.0 convolution_multiply_fusion
  954.1 2.9 collective-permute-start.12
  966.7 3.3 collective-permute-start
  970.0 25.4 %collective-permute-done.7 = bf16[4,256,3,1,128]{4,3,2,1,0:T(2,128)(2,1)} collective-permute-done((bf16[4,256,3,1,128]{4,3,2,1,0:T(2,128)(2,1)S(1)}, bf16[4,256,3,1,128]{4,3,2,1,0:T(2,128)(2,1)}, u32[]{:S(2)}, u32[]{:S(2)}) %collective-permute-start.7) | collective-permute-done | bytes 786464 | tf_op jit(solution)/shard_map/ppermute | solution.py:345
  995.4 4.3 copy_add_fusion
  1003.8 3.1 collective-permute-start.2
  1013.3 7.1 collective-permute-done.9
  1025.3 3.0 collective-permute-done.6
  (325 shorter events, 109.5 us)
Async XLA Ops:
  7.2 477.8 %copy-start = (bf16[512,2048]{1,0:T(8,128)(2,1)S(1)}, bf16[512,2048]{1,0:T(8,128)(2,1)}, u32[]{:S(2)}) copy-start(bf16[512,2048]{1,0:T(8,128)(2,1)} %param.28) | copy-start | bytes 6291460
  16.7 155.0 %all-to-all-start = ((bf16[16,128,1,2048]{3,1,2,0:T(8,128)(2,1)}), bf16[16,128,1,2048]{3,1,2,0:T(8,128)(2,1)}, u32[]{:S(2)}, u32[]{:S(2)}) async-start(bf16[16,128,1,2048]{3,1,2,0:T(8,128)(2,1)} %stack.10), calls=%async_computation | async-start | bytes 16777216 | tf_op jit(solution)/shard_map/all_to_all | solution.py:133
  24.0 314.5 %reduce-scatter.5.cloned.1.call-start = ((), (), s32[]{:S(2)}) async-start(), calls=%async_computation.5 | async-start | bytes 17825792 | tf_op jit(solution)/shard_map/reduce_scatter | solution.py:168
  27.3 768.1 %copy-start.47 = (s32[512]{0:T(512)}, s32[512]{0:T(512)S(1)}, u32[]{:S(2)}) copy-start(s32[512]{0:T(512)S(1)} %iota_add_fusion.2) | copy-start | bytes 6148
  27.3 768.1 %copy-start.45 = (s32[512]{0:T(512)}, s32[512]{0:T(512)S(1)}, u32[]{:S(2)}) copy-start(s32[512]{0:T(512)S(1)} %iota_add_fusion) | copy-start | bytes 6148
  191.7 24.4 %copy-start.27 = (bf16[512,128]{1,0:T(8,128)(2,1)}, bf16[512,128]{1,0:T(8,128)(2,1)S(1)}, u32[]{:S(2)}) copy-start(bf16[512,128]{1,0:T(8,128)(2,1)S(1)} %convert_element_type.283) | copy-start | bytes 393220
  224.2 114.4 %copy-start.58 = (f32[2048]{0:T(1024)S(1)}, f32[2048]{0:T(1024)}, u32[]{:S(2)}) copy-start(f32[2048]{0:T(1024)} %param.23) | copy-start | bytes 24580
  224.2 116.2 %copy-start.43 = (f32[2048]{0:T(1024)S(1)}, f32[2048]{0:T(1024)}, u32[]{:S(2)}) copy-start(f32[2048]{0:T(1024)} %param.24) | copy-start | bytes 24580
  224.2 116.2 %copy-start.59 = (f32[2048]{0:T(1024)S(1)}, f32[2048]{0:T(1024)}, u32[]{:S(2)}) copy-start(f32[2048]{0:T(1024)} %param.25) | copy-start | bytes 24580
  224.3 187.7 %all-gather.4.cloned.1.call-start = ((), (), s32[]{:S(2)}) async-start(), calls=%async_computation.6 | async-start | bytes 8912896 | tf_op jit(solution)/shard_map/all_gather | solution.py:178
  341.5 143.5 %all-gather.6.cloned.1.call-start = ((), (), s32[]{:S(2)}) async-start(), calls=%async_computation.8 | async-start | bytes 8912896 | tf_op jit(solution)/shard_map/all_gather | solution.py:204
  344.3 140.7 %copy-start.72 = (f32[512]{0:T(512)S(1)}, f32[512]{0:T(512)}, u32[]{:S(2)}) copy-start(f32[512]{0:T(512)} %param.27) | copy-start | bytes 6148
  344.3 273.4 %reduce-scatter.9.cloned.1.call-start = ((), (), s32[]{:S(2)}) async-start(), calls=%async_computation.9 | async-start | bytes 17825792 | tf_op jit(solution)/shard_map/reduce_scatter | solution.py:220
  507.3 198.3 %reduce-scatter.7.cloned.1.call-start = ((), (), s32[]{:S(2)}) async-start(), calls=%async_computation.7 | async-start | bytes 8912896 | tf_op jit(solution)/shard_map/reduce_scatter | solution.py:190
  517.6 188.0 %copy-start.60 = (f32[2048]{0:T(1024)S(1)}, f32[2048]{0:T(1024)}, u32[]{:S(2)}) copy-start(f32[2048]{0:T(1024)} %param.29) | copy-start | bytes 24580
  517.6 190.5 %copy-start.21 = (bf16[128,1,2048]{2,0,1:T(8,128)(2,1)S(1)}, bf16[128,1,2048]{2,0,1:T(8,128)(2,1)}, u32[]{:S(2)}) copy-start(bf16[128,1,2048]{2,0,1:T(8,128)(2,1)} %get-tuple-element.79) | copy-start | bytes 1572868
  517.6 261.8 %all-gather.8.cloned.1.call-start = ((), (), s32[]{:S(2)}) async-start(), calls=%async_computation.10 | async-start | bytes 8912896 | tf_op jit(solution)/shard_map/all_gather | solution.py:232
  709.3 252.4 %reduce-scatter.11.cloned.1.call-start = ((), (), s32[]{:S(2)}) async-start(), calls=%async_computation.11 | async-start | bytes 8912896 | tf_op jit(solution)/shard_map/reduce_scatter | solution.py:252
  713.7 81.8 %copy-start.49 = (f32[512]{0:T(512)}, f32[512]{0:T(512)S(1)}, u32[]{:S(2)}) copy-start(f32[512]{0:T(512)S(1)} %get-tuple-element.118) | copy-start | bytes 6148
  713.7 81.8 %copy-start.51 = (f32[512]{0:T(512)}, f32[512]{0:T(512)S(1)}, u32[]{:S(2)}) copy-start(f32[512]{0:T(512)S(1)} %get-tuple-element.117) | copy-start | bytes 6148
  714.2 65.2 %copy-start.38 = (bf16[1,128,2048]{2,1,0:T(8,128)(2,1)S(1)}, bf16[1,128,2048]{2,1,0:T(8,128)(2,1)}, u32[]{:S(2)}) copy-start(bf16[1,128,2048]{2,1,0:T(8,128)(2,1)} %param.22) | copy-start | bytes 1572868
  716.4 79.1 %copy-start.53 = (f32[512]{0:T(512)}, f32[512]{0:T(512)S(1)}, u32[]{:S(2)}) copy-start(f32[512]{0:T(512)S(1)} %get-tuple-element.119) | copy-start | bytes 6148
  716.4 79.1 %copy-start.55 = (f32[512]{0:T(512)}, f32[512]{0:T(512)S(1)}, u32[]{:S(2)}) copy-start(f32[512]{0:T(512)S(1)} %get-tuple-element.120) | copy-start | bytes 6148
  866.3 26.3 %collective-permute-start.13 = (bf16[4,256,512]{2,1,0:T(8,128)(2,1)}, bf16[4,256,512]{2,1,0:T(8,128)(2,1)S(1)}, u32[]{:S(2)}, u32[]{:S(2)}) collective-permute-start(bf16[4,256,512]{2,1,0:T(8,128)(2,1)} %bitcast.58), channel_id=1, source_target_pairs={{0,64},{32,96},{64,0},{96,32},{1,65},{33,97},{65,1},{97,33},{2,66}... | collective-permute-start | bytes 3145736 | tf_op jit(solution)/shard_map/ppermute | solution.py:345
  871.4 42.6 %collective-permute-start.16 = (bf16[512,4,256]{2,0,1:T(8,128)(2,1)}, bf16[512,4,256]{2,0,1:T(8,128)(2,1)}, u32[]{:S(2)}, u32[]{:S(2)}) collective-permute-start(bf16[512,4,256]{2,0,1:T(8,128)(2,1)} %select_convert_fusion), channel_id=1, source_target_pairs={{0,64},{32,96},{64,0},{96,32},{1,65},{33,97},{65,1},{97,33},{2,66}... | collective-permute-start | bytes 3145736 | tf_op jit(solution)/shard_map/ppermute | solution.py:345
  875.6 38.4 %copy-start.13 = (f32[512,4,256]{2,1,0:T(4,128)S(1)}, f32[512,4,256]{2,1,0:T(4,128)}, u32[]{:S(2)}) copy-start(f32[512,4,256]{2,1,0:T(4,128)} %copy-done.12) | copy-start | bytes 6291460
  893.0 23.1 %collective-permute-start.14 = (bf16[2,256,512]{2,1,0:T(8,128)(2,1)S(1)}, bf16[2,256,512]{2,1,0:T(8,128)(2,1)S(1)}, u32[]{:S(2)}, u32[]{:S(2)}) collective-permute-start(bf16[2,256,512]{2,1,0:T(8,128)(2,1)S(1)} %select_convert_fusion.4), channel_id=1, source_target_pairs={{0,32},{32,0},{64,96},{96,64},{1,33},{33,1},{65,97},{97,65},{2,34}... | collective-permute-start | bytes 1572872 | tf_op jit(solution)/shard_map/ppermute | solution.py:345
  916.1 3.7 collective-permute-start.17
  916.5 10.7 %collective-permute-start.15 = (bf16[1,256,512]{2,1,0:T(8,128)(2,1)S(1)}, bf16[1,256,512]{2,1,0:T(8,128)(2,1)S(1)}, u32[]{:S(2)}, u32[]{:S(2)}) collective-permute-start(bf16[1,256,512]{2,1,0:T(8,128)(2,1)S(1)} %select_convert_fusion.6), channel_id=1, source_target_pairs={{0,16},{16,0},{1,17},{17,1},{2,18},{18,2},{3,19},{19,3},{4,20},{20... | collective-permute-start | bytes 786440 | tf_op jit(solution)/shard_map/ppermute | solution.py:345
  920.8 11.7 %collective-permute-start.18 = (bf16[512,1,256]{2,0,1:T(8,128)(2,1)}, bf16[512,1,256]{2,0,1:T(8,128)(2,1)S(1)}, u32[]{:S(2)}, u32[]{:S(2)}) collective-permute-start(bf16[512,1,256]{2,0,1:T(8,128)(2,1)} %select_convert_fusion.5), channel_id=1, source_target_pairs={{0,16},{16,0},{1,17},{17,1},{2,18},{18,2},{3,19},{19,3},{4,20},{20... | collective-permute-start | bytes 786440 | tf_op jit(solution)/shard_map/ppermute | solution.py:345
  941.5 10.1 collective-permute-start.10
  952.0 1.4 collective-permute-start.11
  954.1 6.1 collective-permute-start.12
  959.0 36.4 %collective-permute-start.7 = (bf16[4,256,3,1,128]{4,3,2,1,0:T(2,128)(2,1)S(1)}, bf16[4,256,3,1,128]{4,3,2,1,0:T(2,128)(2,1)}, u32[]{:S(2)}, u32[]{:S(2)}) collective-permute-start(bf16[4,256,3,1,128]{4,3,2,1,0:T(2,128)(2,1)S(1)} %copy.72), channel_id=1, source_target_pairs={{0,64},{32,96},{64,0},{96,32},{1,65},{33,97},{65,1},{97,33},{2,66}... | collective-permute-start | bytes 2359304 | tf_op jit(solution)/shard_map/ppermute | solution.py:345
  966.7 33.0 %collective-permute-start = (f32[8,8,192]{2,0,1:T(8,128)S(1)}, f32[8,8,192]{2,0,1:T(8,128)S(1)}, u32[]{:S(2)}, u32[]{:S(2)}) collective-permute-start(f32[8,8,192]{2,0,1:T(8,128)S(1)} %slice_select_fusion.2), channel_id=1, source_target_pairs={{0,8},{1,9},{2,10},{3,11},{4,12},{5,13},{6,14},{7,15},{8,0},{9,1},... | collective-permute-start | bytes 147464 | tf_op jit(solution)/shard_map/ppermute | solution.py:345
  999.7 24.2 %copy-start.20 = (f32[128,1,2048]{2,0,1:T(8,128)S(1)}, f32[128,1,2048]{2,0,1:T(8,128)}, u32[]{:S(2)}) copy-start(f32[128,1,2048]{2,0,1:T(8,128)} %copy-done.19) | copy-start | bytes 3145732
  999.7 24.2 %copy-start.22 = (bf16[128,1,2048]{2,0,1:T(8,128)(2,1)S(1)}, bf16[128,1,2048]{2,0,1:T(8,128)(2,1)}, u32[]{:S(2)}) copy-start(bf16[128,1,2048]{2,0,1:T(8,128)(2,1)} %get-tuple-element.79) | copy-start | bytes 1572868
  999.7 24.2 %copy-start.23 = (bf16[128,1,2048]{2,0,1:T(8,128)(2,1)S(1)}, bf16[128,1,2048]{2,0,1:T(8,128)(2,1)}, u32[]{:S(2)}) copy-start(bf16[128,1,2048]{2,0,1:T(8,128)(2,1)} %reduce-scatter.11.cloned.1.call-done) | copy-start | bytes 1572868
  999.7 24.2 %copy-start.65 = (f32[128]{0:T(128)S(1)}, f32[128]{0:T(128)}, u32[]{:S(2)}) copy-start(f32[128]{0:T(128)} %copy-done.64) | copy-start | bytes 1540
  999.8 4.0 collective-permute-start.1
  1002.1 4.8 collective-permute-start.8
  1003.8 26.2 %copy-start.1 = (bf16[512,2048]{1,0:T(8,128)(2,1)S(1)}, bf16[512,2048]{1,0:T(8,128)(2,1)}, u32[]{:S(2)}) copy-start(bf16[512,2048]{1,0:T(8,128)(2,1)} %param.28) | copy-start | bytes 6291460
  1003.8 5.3 collective-permute-start.2
  1009.2 3.7 collective-permute-start.3
  1011.1 9.4 collective-permute-start.9
  1012.9 8.9 collective-permute-start.4
  1021.9 1.2 collective-permute-start.5
  1023.1 5.2 collective-permute-start.6
  (56 other events, 408.3 us)
Sparse Core Ops, SparseCore 0:
  224.4 114.1 reduce-scatter.4
  341.7 70.2 all-gather.3
  414.7 70.3 all-gather.5
  507.4 110.2 reduce-scatter.8
  621.0 84.5 reduce-scatter.6
  709.4 69.9 all-gather.7
  843.9 84.3 reduce-scatter.10
